TPU v7x, 512 devices: a whole 4x8x8 slice. The times are simulated.
512 devices in a mesh: bank: 8 (over x, core), gal: 64 (over z, y).
Axes of the slice: x: 4, y: 8, z: 8, core: 2. Of those that a mesh axis runs over, the one named last changes fastest.
Arguments:
- bank_queries: bfloat16 [4096, 768], P(('bank', 'gal'))
- gallery: bfloat16 [262144, 768], P('gal')
- test_queries: bfloat16 [2048, 768], P(('bank', 'gal'))
- test_slabs: int32 [2048, 8], P('bank'), may hold values from 0 to 63, all different within a row; in each aligned block of 4 rows (0 to 3, 4 to 7, ...) at most 2 rows name the same one
- test_offsets: int32 [2048, 8], P('bank'), may hold values from 0 to 31
Outputs:
- pooled: float32 [2048, 768], P(('bank', 'gal'))
Inputs may be any that keep to these rules, and one draw needn't show every extreme that they name: `test_slabs`: each row names 8 different slabs; the 4 rows of one device name no slab more than 2 times, and on some devices one slab exactly 2 times.
All inputs are finite; a program needn't handle non-finite values.
Results may differ from a plain program's by a relative error of at most 0.0065.
Values may be sent and summed in bfloat16 or wider, within the bound.
A program may use at most 64 MiB of HBM per device.

v0:
```python
import jax
import jax.numpy as jnp
from jax import lax
from jax.sharding import PartitionSpec as P

BLOCK = 128
SHARPNESS = 20.0
epsilon = 1e-06


def row_scale(matrix):
    values = matrix.astype(jnp.float32)
    return lax.rsqrt(jnp.sum(values * values, axis=1) + epsilon)


def inner_rows(first_rows, second_rows):
    return lax.dot_general(
        first_rows, second_rows, (((1,), (1,)), ((), ())), preferred_element_type=jnp.float32
    )


def body(bank_queries, gallery, test_queries, test_slabs, test_offsets):
    gallery_rows = gallery.shape[0]
    gallery_scale = row_scale(gallery)
    portion = lax.all_gather(bank_queries, "gal", axis=0, tiled=True)
    scores = (
        SHARPNESS
        * inner_rows(portion, gallery)
        * row_scale(portion)[:, None]
        * gallery_scale[None, :]
    )
    partial_sums = jnp.sum(jnp.exp(scores), axis=0)
    colsum = lax.psum(partial_sums, "bank")
    log_col = jnp.log(colsum)
    own_rows = test_queries.shape[0]
    slab_index = lax.axis_index("gal")
    queries = lax.all_gather(test_queries, "gal", axis=0, tiled=True)
    blocks_here = gallery_rows // BLOCK
    local_blocks = jnp.arange(blocks_here, dtype=jnp.int32)
    block_hits = (test_slabs == slab_index)[:, :, None] & (
        test_offsets[:, :, None] == local_blocks[None, None, :]
    )
    listed = jnp.any(block_hits, axis=1)
    row_mask = jnp.repeat(listed, BLOCK, axis=1)
    logits = (
        SHARPNESS
        * inner_rows(queries, gallery)
        * row_scale(queries)[:, None]
        * gallery_scale[None, :]
        - log_col[None, :]
    )
    weights = jnp.where(row_mask, jnp.exp(logits), jnp.float32(0.0))
    numerator = jnp.dot(weights.astype(jnp.bfloat16), gallery, preferred_element_type=jnp.float32)
    numerator, denominator = (numerator, jnp.sum(weights, axis=1))
    numer_all, denom_all = lax.psum((numerator, denominator), "gal")
    offset = slab_index * own_rows
    numer_own = lax.dynamic_slice_in_dim(numer_all, offset, own_rows, 0)
    denom_own = lax.dynamic_slice_in_dim(denom_all, offset, own_rows, 0)
    return numer_own / denom_own[:, None]


def solution(mesh):
    in_specs = (
        P(("bank", "gal"), None),
        P("gal", None),
        P(("bank", "gal"), None),
        P("bank", None),
        P("bank", None),
    )
    out_specs = P(("bank", "gal"), None)
    return jax.shard_map(body, mesh=mesh, in_specs=in_specs, out_specs=out_specs, check_vma=False)
```

profile of v0, /device:TPU:2, one launch (start us, length us, event | category | flops | bytes accessed | tf_op | source)
XLA Modules:
  0.0 317.6 jit_solution(15684312714763030671)
XLA Ops:
  6.5 0.0 copy-start.1
  6.5 0.0 copy-start.2
  6.5 0.0 copy-start.3
  6.5 0.0 copy-start
  6.5 0.0 all-reduce.2.cloned.1.call-start
  6.6 4.1 %multiply_reduce_fusion = f32[4096]{0:T(1024)S(1)} fusion(bf16[4096,768]{1,0:T(8,128)(2,1)} %param.6), kind=kLoop, calls=%fused_computation | loop fusion | flops 9433088 | bytes 6307840 | tf_op jit(solution)/shard_map/reduce_sum | solution.py:13
  10.7 0.0 copy-done.1
  10.7 0.0 copy-done.2
  10.8 0.1 copy.10
  10.9 0.0 copy-done.3
  10.9 56.8 %all-gather = bf16[64,4,768]{2,1,0:T(4,128)(2,1)S(1)} all-gather(bf16[1,4,768]{2,1,0:T(4,128)(2,1)S(1)} %bitcast.13), channel_id=1, replica_groups=mesh['bank'=8,'gal'=64] {'gal'}, dimensions={0}, use_global_device_ids=true | all-gather | bytes 399360 | tf_op jit(solution)/shard_map/all_gather | solution.py:37
  67.7 0.1 reshape.21
  67.8 0.2 multiply_reduce_fusion.2
  68.0 0.0 copy-done
  68.0 48.5 %all_gather.7 = bf16[512,768]{1,0:T(8,128)(2,1)S(1)} all-gather(bf16[8,768]{1,0:T(8,128)(2,1)S(1)} %copy-done), channel_id=1, replica_groups=mesh['bank'=8,'gal'=64] {'gal'}, dimensions={0}, use_global_device_ids=true | all-gather | bytes 798720 | tf_op jit(solution)/shard_map/all_gather | solution.py:25
  116.5 0.2 multiply_reduce_fusion.1
  116.8 6.5 %exponential_reduce_fusion = f32[4096]{0:T(1024)S(1)} fusion(bf16[512,768]{1,0:T(8,128)(2,1)S(1)} %all_gather.7, bf16[4096,768]{1,0:T(8,128)(2,1)} %param.6, f32[4096]{0:T(1024)S(1)} %add_rsqrt_fusion, f32[512]{0:T(512)S(1)} %rsqrt_multiply_fusion), kind=kOutput, calls=%fused_computation.1 | convolution fusion | flops 3227512832 | bytes 7112704 | tf_op jit(solution)/shard_map/dot_general | solution.py:17
  123.3 20.6 %psum.21 = f32[4096]{0:T(1024)S(1)} all-reduce(f32[4096]{0:T(1024)S(1)} %exponential_reduce_fusion), channel_id=1, replica_groups=mesh['bank'=8,'gal'=64] {'bank'}, use_global_device_ids=true, to_apply=%region_5.0 | all-reduce | flops 4096 | bytes 32768 | tf_op jit(solution)/shard_map/psum | solution.py:33
  143.9 0.0 slice-start
  143.9 2.1 broadcast_in_dim.5
  146.0 0.0 slice-start.1
  146.0 5.3 %fusion.8 = (f32[256]{0:T(256)S(1)}, bf16[256,4096]{1,0:T(8,128)(2,1)S(1)}) fusion(f32[4096]{0:T(1024)S(1)} %log.3, f32[4096]{0:T(1024)S(1)} %add_rsqrt_fusion, f32[256]{0:T(256)S(1)} %rsqrt_multiply_fusion.1, bf16[256,768]{1,0:T(8,128)(2,1)S(1)} %reshape.21, bf16[4096,768]{1,0:T(8,128)(2,1)} %param.6, pred[32,8,32,128]{3,2,1,0:T(32,128)(4,1)S(1)} %bitcast.12), kind=kOutput, calls=%fused_computation.19 | convolution fusion | flops 1616903936 | bytes 9865216 | tf_op jit(solution)/shard_map/dot_general | solution.py:17
  151.3 0.0 slice-done
  151.3 0.0 slice-done.1
  151.4 2.7 fusion.4
  154.1 0.0 all-reduce.2.cloned.1.call-update
  154.1 140.7 %psum.23 = f32[256]{0:T(256)S(1)} all-reduce(f32[256]{0:T(256)S(1)} %get-tuple-element.5), channel_id=1, replica_groups=mesh['bank'=8,'gal'=64] {'gal'}, use_global_device_ids=true, to_apply=%region_8.9 | all-reduce | flops 256 | bytes 2048 | tf_op jit(solution)/shard_map/psum | solution.py:55
  294.8 0.1 dynamic_slice.7
  294.9 14.5 %all-reduce.2.cloned.1.call-done = f32[256,768]{1,0:T(8,128)} async-done(((f32[256,768]{1,0:T(8,128)}), f32[256,768]{1,0:T(8,128)}) %all-reduce.2.cloned.1.call-update) | async-done | bytes 786448 | tf_op jit(solution)/shard_map/psum | solution.py:55
  309.4 1.4 dynamic-slice_divide_fusion
  (7 shorter events, 0.1 us)
Async XLA Ops:
  6.5 4.2 %copy-start.1 = (s32[256,8]{0,1:T(8,128)S(1)}, s32[256,8]{0,1:T(8,128)}, u32[]{:S(2)}) copy-start(s32[256,8]{0,1:T(8,128)} %param.8) | copy-start | bytes 24580
  6.5 4.2 %copy-start.2 = (s32[256,8]{0,1:T(8,128)S(1)}, s32[256,8]{0,1:T(8,128)}, u32[]{:S(2)}) copy-start(s32[256,8]{0,1:T(8,128)} %param.9) | copy-start | bytes 24580
  6.5 4.4 %copy-start.3 = (bf16[4,768]{1,0:T(4,128)(2,1)S(1)}, bf16[4,768]{1,0:T(4,128)(2,1)}, u32[]{:S(2)}) copy-start(bf16[4,768]{1,0:T(4,128)(2,1)} %param.7) | copy-start | bytes 18436
  6.5 61.5 %copy-start = (bf16[8,768]{1,0:T(8,128)(2,1)S(1)}, bf16[8,768]{1,0:T(8,128)(2,1)}, u32[]{:S(2)}) copy-start(bf16[8,768]{1,0:T(8,128)(2,1)} %param.5) | copy-start | bytes 36868
  6.5 302.8 %all-reduce.2.cloned.1.call-start = ((), (), s32[]{:S(2)}) async-start(), calls=%async_computation | async-start | bytes 1572864 | tf_op jit(solution)/shard_map/psum | solution.py:55
  143.9 7.4 %slice-start = ((s8[6291456]{0:T(1024)(128)(4,1)}), s8[4194304]{0:T(1024)(128)(4,1)S(1)}, s32[]{:S(2)}) async-start(s8[6291456]{0:T(1024)(128)(4,1)} %bitcast.10), calls=%async_computation.1 | async-start | bytes 8388608
  146.0 5.3 %slice-start.1 = ((s8[6291456]{0:T(1024)(128)(4,1)}), s8[2097152]{0:T(1024)(128)(4,1)S(1)}, s32[]{:S(2)}) async-start(s8[6291456]{0:T(1024)(128)(4,1)} %bitcast.10), calls=%async_computation.2 | async-start | bytes 4194304
Sparse Core Ops, SparseCore 0:
  154.2 155.1 all-reduce.1
where the time goes:
time: 318 us
  blocking collectives  267 us (84%)
  matrix products  14.6 us (5%)
  waiting for transfers between devices  14.5 us (5%)
  between operations  13.5 us (4%)
  other arithmetic  5.96 us (2%)
    psum x1, blocking collectives, body(): numer_all, denom_all = lax.psum((numerator, denominator), 'gal')  141 us
    all_gather x1, blocking collectives, body(): queries = lax.all_gather(test_queries, 'gal', axis=0, tiled=True)  56.8 us
    all_gather x1, blocking collectives, body(): portion = lax.all_gather(bank_queries, 'gal', axis=0, tiled=True)  48.5 us
    psum x1, blocking collectives, body(): colsum = lax.psum(partial_sums, 'bank')  20.6 us
    psum x1, waiting for transfers between devices, body(): numer_all, denom_all = lax.psum((numerator, denominator), 'gal')  14.5 us
    dot_general x2, matrix products, inner_rows(): lax.dot_general(first_rows, second_rows, (((1,), (1,)), ((), ())), prefer...  11.8 us
  transfers between devices with their start and end apart: 1, of which 1 were waited for; matrix products, arithmetic and copies ran while one was open for 0% of the time, Pallas kernels for 0%

commit v1 on v0

--- a/solution.py
+++ b/solution.py
@@ -30,7 +30,7 @@
         * gallery_scale[None, :]
     )
     partial_sums = jnp.sum(jnp.exp(scores), axis=0)
-    colsum = lax.psum(partial_sums, "bank")
+    colsum = jnp.sum(lax.all_gather(partial_sums, "bank"), axis=0)
     log_col = jnp.log(colsum)
     own_rows = test_queries.shape[0]
     slab_index = lax.axis_index("gal")

time: 318 us -> 309 us (0.972)
  blocking collectives: 267 us -> 259 us
    psum x1 -> x0, blocking collectives: 20.6 us -> none  [body(): colsum = lax.psum(partial_sums, 'bank')]
    all_gather x0 -> x1, blocking collectives: none -> 12.8 us  [body(): colsum = jnp.sum(lax.all_gather(partial_sums, 'bank'), axis=0)]
where the time goes in v1:
time: 309 us
  blocking collectives  259 us (84%)
  matrix products  14.6 us (5%)
  waiting for transfers between devices  13.8 us (4%)
  between operations  13.6 us (4%)
  other arithmetic  6 us (2%)
    psum x1, blocking collectives, body(): numer_all, denom_all = lax.psum((numerator, denominator), 'gal')  141 us
    all_gather x1, blocking collectives, body(): queries = lax.all_gather(test_queries, 'gal', axis=0, tiled=True)  56.8 us
    all_gather x1, blocking collectives, body(): portion = lax.all_gather(bank_queries, 'gal', axis=0, tiled=True)  48.5 us
    psum x1, waiting for transfers between devices, body(): numer_all, denom_all = lax.psum((numerator, denominator), 'gal')  13.8 us
    all_gather x1, blocking collectives, body(): colsum = jnp.sum(lax.all_gather(partial_sums, 'bank'), axis=0)  12.8 us
    dot_general x2, matrix products, inner_rows(): lax.dot_general(first_rows, second_rows, (((1,), (1,)), ((), ())), prefer...  11.8 us
  transfers between devices with their start and end apart: 1, of which 1 were waited for; matrix products, arithmetic and copies ran while one was open for 0% of the time, Pallas kernels for 0%

profile of v1, /device:TPU:2, one launch (start us, length us, event | category | flops | bytes accessed | tf_op | source)
XLA Modules:
  0.0 309.1 jit_solution(16837567404909940524)
XLA Ops:
  6.5 0.0 copy-start.1
  6.5 0.0 copy-start.2
  6.5 0.0 copy-start.3
  6.5 0.0 copy-start
  6.5 0.0 all-reduce.2.cloned.1.call-start
  6.6 4.1 %multiply_reduce_fusion = f32[4096]{0:T(1024)S(1)} fusion(bf16[4096,768]{1,0:T(8,128)(2,1)} %param.6), kind=kLoop, calls=%fused_computation | loop fusion | flops 9433088 | bytes 6307840 | tf_op jit(solution)/shard_map/reduce_sum | solution.py:13
  10.7 0.0 copy-done.1
  10.7 0.0 copy-done.2
  10.8 0.1 copy.10
  10.9 0.0 copy-done.3
  10.9 56.8 %all-gather.1 = bf16[64,4,768]{2,1,0:T(4,128)(2,1)S(1)} all-gather(bf16[1,4,768]{2,1,0:T(4,128)(2,1)S(1)} %bitcast.13), channel_id=1, replica_groups=mesh['bank'=8,'gal'=64] {'gal'}, dimensions={0}, use_global_device_ids=true | all-gather | bytes 399360 | tf_op jit(solution)/shard_map/all_gather | solution.py:37
  67.7 0.1 reshape.24
  67.8 0.2 multiply_reduce_fusion.2
  68.0 0.0 copy-done
  68.0 48.5 %all_gather.13 = bf16[512,768]{1,0:T(8,128)(2,1)S(1)} all-gather(bf16[8,768]{1,0:T(8,128)(2,1)S(1)} %copy-done), channel_id=1, replica_groups=mesh['bank'=8,'gal'=64] {'gal'}, dimensions={0}, use_global_device_ids=true | all-gather | bytes 798720 | tf_op jit(solution)/shard_map/all_gather | solution.py:25
  116.5 0.2 multiply_reduce_fusion.1
  116.8 6.5 %exponential_reduce_fusion = f32[4096]{0:T(1024)S(1)} fusion(bf16[512,768]{1,0:T(8,128)(2,1)S(1)} %all_gather.13, bf16[4096,768]{1,0:T(8,128)(2,1)} %param.6, f32[4096]{0:T(1024)S(1)} %add_rsqrt_fusion, f32[512]{0:T(512)S(1)} %rsqrt_multiply_fusion), kind=kOutput, calls=%fused_computation.1 | convolution fusion | flops 3227512832 | bytes 7112704 | tf_op jit(solution)/shard_map/dot_general | solution.py:17
  123.3 12.8 %all-gather = f32[32768]{0:T(1024)S(1)} all-gather(f32[4096]{0:T(1024)S(1)} %exponential_reduce_fusion), channel_id=2, replica_groups=mesh['bank'=8,'gal'=64] {'bank'}, dimensions={0}, use_global_device_ids=true | all-gather | bytes 147456 | tf_op jit(solution)/shard_map/all_gather | solution.py:33
  136.2 0.0 slice-start
  136.2 2.1 broadcast_in_dim.5
  138.3 0.0 slice-start.1
  138.3 5.3 %fusion.8 = (f32[256]{0:T(256)S(1)}, bf16[256,4096]{1,0:T(8,128)(2,1)S(1)}) fusion(f32[4096]{0:T(1024)S(1)} %log.7, f32[4096]{0:T(1024)S(1)} %add_rsqrt_fusion, f32[256]{0:T(256)S(1)} %rsqrt_multiply_fusion.1, bf16[256,768]{1,0:T(8,128)(2,1)S(1)} %reshape.24, bf16[4096,768]{1,0:T(8,128)(2,1)} %param.6, pred[32,8,32,128]{3,2,1,0:T(32,128)(4,1)S(1)} %bitcast.12), kind=kOutput, calls=%fused_computation.19 | convolution fusion | flops 1616903936 | bytes 9865216 | tf_op jit(solution)/shard_map/dot_general | solution.py:17
  143.6 0.0 slice-done
  143.6 0.0 slice-done.1
  143.6 2.7 fusion.4
  146.3 0.0 all-reduce.2.cloned.1.call-update
  146.4 140.6 %psum.15 = f32[256]{0:T(256)S(1)} all-reduce(f32[256]{0:T(256)S(1)} %get-tuple-element.5), channel_id=1, replica_groups=mesh['bank'=8,'gal'=64] {'gal'}, use_global_device_ids=true, to_apply=%region_8.9 | all-reduce | flops 256 | bytes 2048 | tf_op jit(solution)/shard_map/psum | solution.py:55
  287.0 0.1 dynamic_slice.7
  287.1 13.8 %all-reduce.2.cloned.1.call-done = f32[256,768]{1,0:T(8,128)} async-done(((f32[256,768]{1,0:T(8,128)}), f32[256,768]{1,0:T(8,128)}) %all-reduce.2.cloned.1.call-update) | async-done | bytes 786448 | tf_op jit(solution)/shard_map/psum | solution.py:55
  300.8 1.4 dynamic-slice_divide_fusion
  (9 shorter events, 0.1 us)
Async XLA Ops:
  6.5 4.2 %copy-start.1 = (s32[256,8]{0,1:T(8,128)S(1)}, s32[256,8]{0,1:T(8,128)}, u32[]{:S(2)}) copy-start(s32[256,8]{0,1:T(8,128)} %param.8) | copy-start | bytes 24580
  6.5 4.2 %copy-start.2 = (s32[256,8]{0,1:T(8,128)S(1)}, s32[256,8]{0,1:T(8,128)}, u32[]{:S(2)}) copy-start(s32[256,8]{0,1:T(8,128)} %param.9) | copy-start | bytes 24580
  6.5 4.4 %copy-start.3 = (bf16[4,768]{1,0:T(4,128)(2,1)S(1)}, bf16[4,768]{1,0:T(4,128)(2,1)}, u32[]{:S(2)}) copy-start(bf16[4,768]{1,0:T(4,128)(2,1)} %param.7) | copy-start | bytes 18436
  6.5 61.5 %copy-start = (bf16[8,768]{1,0:T(8,128)(2,1)S(1)}, bf16[8,768]{1,0:T(8,128)(2,1)}, u32[]{:S(2)}) copy-start(bf16[8,768]{1,0:T(8,128)(2,1)} %param.5) | copy-start | bytes 36868
  6.5 294.3 %all-reduce.2.cloned.1.call-start = ((), (), s32[]{:S(2)}) async-start(), calls=%async_computation | async-start | bytes 1572864 | tf_op jit(solution)/shard_map/psum | solution.py:55
  136.2 7.4 %slice-start = ((s8[6291456]{0:T(1024)(128)(4,1)}), s8[4194304]{0:T(1024)(128)(4,1)S(1)}, s32[]{:S(2)}) async-start(s8[6291456]{0:T(1024)(128)(4,1)} %bitcast.10), calls=%async_computation.1 | async-start | bytes 8388608
  138.3 5.3 %slice-start.1 = ((s8[6291456]{0:T(1024)(128)(4,1)}), s8[2097152]{0:T(1024)(128)(4,1)S(1)}, s32[]{:S(2)}) async-start(s8[6291456]{0:T(1024)(128)(4,1)} %bitcast.10), calls=%async_computation.2 | async-start | bytes 4194304
Sparse Core Ops, SparseCore 0:
  146.5 154.3 all-reduce.1

commit v2 on v0

--- a/solution.py
+++ b/solution.py
@@ -22,7 +22,9 @@
 def body(bank_queries, gallery, test_queries, test_slabs, test_offsets):
     gallery_rows = gallery.shape[0]
     gallery_scale = row_scale(gallery)
-    portion = lax.all_gather(bank_queries, "gal", axis=0, tiled=True)
+    portion = jnp.concatenate(
+        lax.all_to_all(jnp.stack([bank_queries] * lax.axis_size("gal")), "gal", 0, 0), axis=0
+    )
     scores = (
         SHARPNESS
         * inner_rows(portion, gallery)

time: 318 us -> 296 us (0.931)
  blocking collectives: 267 us -> 222 us
  starting transfers between devices: 0.03 us -> 16.6 us
  waiting for transfers between devices: 14.5 us -> 18 us
    all_gather x1 -> x0, blocking collectives: 48.5 us -> none  [body(): portion = lax.all_gather(bank_queries, 'gal', axis=0, tiled=True)]
    all_to_all x0 -> x1, starting transfers between devices: none -> 16.6 us  [body(): lax.all_to_all(jnp.stack([bank_queries] * lax.axis_size('gal')), 'gal', 0...]
    all_gather x1, blocking collectives: 56.8 us -> 60.4 us  [body(): queries = lax.all_gather(test_queries, 'gal', axis=0, tiled=True)]
    psum x1, waiting for transfers between devices: 14.5 us -> 17.9 us  [body(): numer_all, denom_all = lax.psum((numerator, denominator), 'gal')]
  transfers between devices with their start and end apart: 1 -> 2, of which waited for: 1 -> 1; matrix products, arithmetic and copies ran while one was open for 0% -> 2% of each run, Pallas kernels for 0% -> 0%
where the time goes in v2:
time: 296 us
  blocking collectives  222 us (75%)
  waiting for transfers between devices  18 us (6%)
  starting transfers between devices  16.6 us (6%)
  matrix products  14.5 us (5%)
  between operations  13.5 us (5%)
  other arithmetic  7.36 us (2%)
  local copies, waits for them, and re-layouts  4.09 us (1%)
    psum x1, blocking collectives, body(): numer_all, denom_all = lax.psum((numerator, denominator), 'gal')  141 us
    all_gather x1, blocking collectives, body(): queries = lax.all_gather(test_queries, 'gal', axis=0, tiled=True)  60.4 us
    psum x1, blocking collectives, body(): colsum = lax.psum(partial_sums, 'bank')  20.6 us
    psum x1, waiting for transfers between devices, body(): numer_all, denom_all = lax.psum((numerator, denominator), 'gal')  17.9 us
    all_to_all x1, starting transfers between devices, body(): lax.all_to_all(jnp.stack([bank_queries] * lax.axis_size('gal')), 'gal', 0...  16.6 us
    dot_general x2, matrix products, inner_rows(): lax.dot_general(first_rows, second_rows, (((1,), (1,)), ((), ())), prefer...  11.8 us
  transfers between devices with their start and end apart: 2, of which 1 were waited for; matrix products, arithmetic and copies ran while one was open for 2% of the time, Pallas kernels for 0%

profile of v2, /device:TPU:2, one launch (start us, length us, event | category | flops | bytes accessed | tf_op | source)
XLA Modules:
  0.0 295.7 jit_solution(6478085900478341852)
XLA Ops:
  6.5 1.6 stack.2
  8.2 16.6 %all-to-all-start = ((bf16[64,8,768]{2,1,0:T(8,128)(2,1)}), bf16[64,8,768]{2,1,0:T(8,128)(2,1)S(1)}, u32[]{:S(2)}, u32[]{:S(2)}) async-start(bf16[64,8,768]{2,1,0:T(8,128)(2,1)} %stack.2), calls=%async_computation | async-start | bytes 1572864 | tf_op jit(solution)/shard_map/all_to_all | solution.py:26
  24.8 0.0 all-reduce.2.cloned.1.call-start
  24.8 0.7 broadcast_compare_fusion
  25.5 0.7 fusion.8
  26.3 0.1 copy.12
  26.4 60.4 %all-gather = bf16[64,4,768]{2,1,0:T(4,128)(2,1)S(1)} all-gather(bf16[1,4,768]{2,1,0:T(4,128)(2,1)} %bitcast.15), channel_id=1, replica_groups=mesh['bank'=8,'gal'=64] {'gal'}, dimensions={0}, use_global_device_ids=true | all-gather | bytes 399360 | tf_op jit(solution)/shard_map/all_gather | solution.py:39
  86.8 0.1 reshape.36
  86.9 0.2 multiply_reduce_fusion.2
  87.1 4.1 %multiply_reduce_fusion = f32[4096]{0:T(1024)S(1)} fusion(bf16[4096,768]{1,0:T(8,128)(2,1)} %param.6), kind=kLoop, calls=%fused_computation | loop fusion | flops 9433088 | bytes 6307840 | tf_op jit(solution)/shard_map/reduce_sum | solution.py:13
  91.2 0.0 all-to-all-done
  91.2 0.2 multiply_reduce_fusion.1
  91.4 0.1 mul.70
  91.5 6.5 %exponential_reduce_fusion = f32[4096]{0:T(1024)S(1)} fusion(bf16[4096,768]{1,0:T(8,128)(2,1)} %param.6, f32[4096]{0:T(1024)S(1)} %add_rsqrt_fusion, f32[512]{0:T(512)S(1)} %mul.70, bf16[64,8,768]{2,1,0:T(8,128)(2,1)S(1)} %all-to-all-done), kind=kOutput, calls=%fused_computation.1 | convolution fusion | flops 3227512832 | bytes 7112704 | tf_op jit(solution)/shard_map/dot_general | solution.py:17
  98.1 20.6 %psum.21 = f32[4096]{0:T(1024)S(1)} all-reduce(f32[4096]{0:T(1024)S(1)} %exponential_reduce_fusion), channel_id=1, replica_groups=mesh['bank'=8,'gal'=64] {'bank'}, use_global_device_ids=true, to_apply=%region_5.0 | all-reduce | flops 4096 | bytes 32768 | tf_op jit(solution)/shard_map/psum | solution.py:35
  118.7 0.0 slice-start
  118.7 2.1 broadcast_in_dim.5
  120.8 0.0 slice-start.1
  120.8 5.3 %fusion.9 = (f32[256]{0:T(256)S(1)}, bf16[256,4096]{1,0:T(8,128)(2,1)S(1)}) fusion(f32[4096]{0:T(1024)S(1)} %log.3, f32[4096]{0:T(1024)S(1)} %add_rsqrt_fusion, f32[256]{0:T(256)S(1)} %rsqrt_multiply_fusion.1, bf16[256,768]{1,0:T(8,128)(2,1)S(1)} %reshape.36, bf16[4096,768]{1,0:T(8,128)(2,1)} %param.6, pred[32,8,32,128]{3,2,1,0:T(32,128)(4,1)S(1)} %bitcast.14), kind=kOutput, calls=%fused_computation.20 | convolution fusion | flops 1616903936 | bytes 9865216 | tf_op jit(solution)/shard_map/dot_general | solution.py:17
  126.0 0.0 slice-done
  126.1 0.0 slice-done.1
  126.1 2.7 fusion.4
  128.8 0.0 all-reduce.2.cloned.1.call-update
  128.8 140.6 %psum.23 = f32[256]{0:T(256)S(1)} all-reduce(f32[256]{0:T(256)S(1)} %get-tuple-element.5), channel_id=1, replica_groups=mesh['bank'=8,'gal'=64] {'gal'}, use_global_device_ids=true, to_apply=%region_8.9 | all-reduce | flops 256 | bytes 2048 | tf_op jit(solution)/shard_map/psum | solution.py:57
  269.4 0.1 dynamic_slice.7
  269.5 17.9 %all-reduce.2.cloned.1.call-done = f32[256,768]{1,0:T(8,128)} async-done(((f32[256,768]{1,0:T(8,128)}), f32[256,768]{1,0:T(8,128)}) %all-reduce.2.cloned.1.call-update) | async-done | bytes 786448 | tf_op jit(solution)/shard_map/psum | solution.py:57
  287.5 1.4 dynamic-slice_divide_fusion
  (5 shorter events, 0.0 us)
Async XLA Ops:
  8.2 83.0 %all-to-all-start = ((bf16[64,8,768]{2,1,0:T(8,128)(2,1)}), bf16[64,8,768]{2,1,0:T(8,128)(2,1)S(1)}, u32[]{:S(2)}, u32[]{:S(2)}) async-start(bf16[64,8,768]{2,1,0:T(8,128)(2,1)} %stack.2), calls=%async_computation | async-start | bytes 1572864 | tf_op jit(solution)/shard_map/all_to_all | solution.py:26
  24.8 262.7 %all-reduce.2.cloned.1.call-start = ((), (), s32[]{:S(2)}) async-start(), calls=%async_computation.1 | async-start | bytes 1572864 | tf_op jit(solution)/shard_map/psum | solution.py:57
  118.7 7.3 %slice-start = ((s8[6291456]{0:T(1024)(128)(4,1)}), s8[4194304]{0:T(1024)(128)(4,1)S(1)}, s32[]{:S(2)}) async-start(s8[6291456]{0:T(1024)(128)(4,1)} %bitcast.12), calls=%async_computation.2 | async-start | bytes 8388608
  120.8 5.3 %slice-start.1 = ((s8[6291456]{0:T(1024)(128)(4,1)}), s8[2097152]{0:T(1024)(128)(4,1)S(1)}, s32[]{:S(2)}) async-start(s8[6291456]{0:T(1024)(128)(4,1)} %bitcast.12), calls=%async_computation.3 | async-start | bytes 4194304
Sparse Core Ops, SparseCore 0:
  128.9 158.4 all-reduce.1
